TPU v7x, 32 devices: a whole 2x2x4 slice. The times are simulated.
32 devices in a mesh: grp: 2 (over x), tok: 4 (over z), head: 4 (over y, core).
Axes of the slice: x: 2, y: 2, z: 4, core: 2. Of those that a mesh axis runs over, the one named last changes fastest.
Arguments:
- views: bfloat16 [2, 2, 768, 1024], P('grp', None, 'tok'), may hold values from -6 to 6
- q_weight: bfloat16 [1024, 1024], P(None, 'head'), may hold values from -0.1875 to 0.1875
- k_weight: bfloat16 [1024, 1024], P(None, 'head'), may hold values from -0.1875 to 0.1875
- v_weight: bfloat16 [1024, 1024], P(None, 'head'), may hold values from -0.1875 to 0.1875
- rate_weight: bfloat16 [1024, 4], P(None, 'head'), may hold values from -0.1875 to 0.1875
- fast_in: float32 [4, 256, 1024], P('head', None, 'tok'), may hold values from -0.375 to 0.375
- fast_out: float32 [4, 512, 256], P('head', None, 'tok'), may hold values from -0.25 to 0.25
- out_gain: float32 [1024], P('head'), may hold values from 0.1 to 1.9
Outputs:
- rendered: bfloat16 [2, 2, 768, 1024], P('grp', None, 'tok', 'head')
All inputs are finite; a program needn't handle non-finite values.
Results may differ from a plain program's by a relative error of at most 0.013.
Values may be sent and summed in bfloat16 or wider, within the bound.
A program may use at most 64 MiB of HBM per device.

v0:
```python
import math
import jax
import jax.numpy as jnp
from jax import lax
from jax.sharding import PartitionSpec as P

norm_eps = 1e-06
out_eps = 1e-05
step_coef = 0.3
momentum_keep = 0.5


def spread(value, axis, source):
    kept = jnp.where(lax.axis_index(axis) == source, value, 0).astype(value.dtype)
    return lax.psum(kept, axis)


def rms_scale(values):
    return values * lax.rsqrt(jnp.mean(values * values, axis=-1, keepdims=True) + norm_eps)


def contract_rows(left, right):
    return lax.dot_general(
        left, right, (((0,), (0,)), ((), ())), preferred_element_type=jnp.float32
    )


def contract_cols(left, right):
    return lax.dot_general(
        left, right, (((1,), (1,)), ((), ())), preferred_element_type=jnp.float32
    )


def fast_apply(queries, copy_in, copy_out):
    hidden_units = copy_out.shape[0]
    pre_act = jnp.dot(queries, copy_in, preferred_element_type=jnp.float32)
    gate = pre_act[:, :hidden_units]
    upper = pre_act[:, hidden_units:]
    hidden = (gate * jax.nn.sigmoid(gate) * upper).astype(jnp.bfloat16)
    return jnp.dot(hidden, copy_out, preferred_element_type=jnp.float32)


def local(views, q_weight, k_weight, v_weight, rate_weight, fast_in, fast_out, out_gain):
    tok_count = lax.axis_size("tok")
    is_input = lax.axis_index("grp") == 0
    spans = views.shape[1]
    head_size = fast_in.shape[1]
    hidden_units = fast_out.shape[1]
    step_size = step_coef / math.sqrt(views.shape[2] * tok_count)
    width_all = head_size * lax.axis_size("head")
    whole_in, whole_out = (
        lax.all_gather(fast_in, "tok", axis=2, tiled=True),
        lax.all_gather(fast_out, "tok", axis=2, tiled=True),
    )
    whole_in = whole_in[0]
    whole_out = whole_out[0]
    copy_in = whole_in.astype(jnp.bfloat16)
    copy_out = whole_out.astype(jnp.bfloat16)
    state_in = fast_in[0]
    state_out = fast_out[0]
    base_in = jnp.mean(state_in * state_in, axis=0, keepdims=True)
    base_out = jnp.mean(state_out * state_out, axis=0, keepdims=True)
    moment_in = jnp.zeros_like(state_in)
    moment_out = jnp.zeros_like(state_out)

    def input_grads(inputs, given_in, given_out):
        keyed = rms_scale(jnp.dot(inputs, k_weight, preferred_element_type=jnp.float32)).astype(
            jnp.bfloat16
        )
        valued = jnp.dot(inputs, v_weight, preferred_element_type=jnp.float32)
        rates = jax.nn.softplus(jnp.dot(inputs, rate_weight, preferred_element_type=jnp.float32))
        upstream = (-(step_size * rates) * valued).astype(jnp.bfloat16)
        pre_act = jnp.dot(keyed, given_in, preferred_element_type=jnp.float32)
        gate = pre_act[:, :hidden_units]
        upper = pre_act[:, hidden_units:]
        sigma = jax.nn.sigmoid(gate)
        active = gate * sigma
        hidden = (active * upper).astype(jnp.bfloat16)
        grad_out = contract_rows(hidden, upstream)
        back = contract_cols(upstream, given_out)
        back_pre = jnp.concatenate(
            [back * upper * sigma * (1.0 + gate * (1.0 - sigma)), back * active], axis=1
        ).astype(jnp.bfloat16)
        grad_in = contract_rows(keyed, back_pre)
        return (grad_in, grad_out)

    def novel_grads(inputs, given_in, given_out):
        return (
            jnp.zeros((head_size, 2 * hidden_units), jnp.float32),
            jnp.zeros((hidden_units, head_size), jnp.float32),
        )

    outputs = []
    for span in range(spans):
        inputs = views[0, span]
        queries = rms_scale(jnp.dot(inputs, q_weight, preferred_element_type=jnp.float32)).astype(
            jnp.bfloat16
        )
        grads = lax.cond(is_input, input_grads, novel_grads, inputs, copy_in, copy_out)
        grad_in, grad_out = lax.psum_scatter(grads, "tok", scatter_dimension=1, tiled=True)
        moment_in = momentum_keep * moment_in + grad_in
        moment_out = momentum_keep * moment_out + grad_out
        trial_in = state_in - moment_in
        trial_out = state_out - moment_out
        mean_in = jnp.mean(trial_in * trial_in, axis=0, keepdims=True)
        mean_out = jnp.mean(trial_out * trial_out, axis=0, keepdims=True)
        state_in = trial_in * jnp.sqrt(base_in) * lax.rsqrt(mean_in + norm_eps)
        state_out = trial_out * jnp.sqrt(base_out) * lax.rsqrt(mean_out + norm_eps)
        part_in = state_in.astype(jnp.bfloat16)
        part_out = state_out.astype(jnp.bfloat16)
        copy_in, copy_out = (
            lax.all_gather(part_in, "tok", axis=1, tiled=True),
            lax.all_gather(part_out, "tok", axis=1, tiled=True),
        )
        copy_in, copy_out = (spread(copy_in, "grp", 0), spread(copy_out, "grp", 0))
        produced = fast_apply(queries, copy_in, copy_out)
        squares = lax.psum(jnp.sum(produced * produced, axis=1), "head")
        normed = produced * lax.rsqrt(squares / width_all + out_eps)[:, None] * out_gain
        outputs.append(normed.astype(jnp.bfloat16))
    return jnp.stack(outputs)[None]


def solution(mesh):
    placed = (
        P("grp", None, "tok", None),
        P(None, "head"),
        P(None, "head"),
        P(None, "head"),
        P(None, "head"),
        P("head", None, "tok"),
        P("head", None, "tok"),
        P("head"),
    )
    return jax.shard_map(
        local, mesh=mesh, in_specs=placed, out_specs=P("grp", None, "tok", "head"), check_vma=False
    )
```

profile of v0, /device:TPU:0, one launch (start us, length us, event | category | flops | bytes accessed | tf_op | source)
XLA Modules:
  0.0 281.3 jit_solution(5273160163596320403)
XLA Ops:
  6.5 1.2 slice_bitcast_fusion.1
  8.0 18.1 %all_gather.18 = bf16[1,512,256]{1,0,2:T(2,128)(2,1)} all-gather(bf16[1,512,64]{1,0,2:T(2,128)(2,1)S(1)} %copy.11), channel_id=1, replica_groups=mesh['grp'=2,'tok'=4,'head'=4] {'tok'}, dimensions={2}, use_global_device_ids=true | all-gather | bytes 327680 | tf_op jit(solution)/shard_map/all_gather | solution.py:53
  26.1 16.5 %all_gather.19 = bf16[1,256,1024]{2,1,0:T(8,128)(2,1)S(1)} all-gather(bf16[1,256,256]{2,1,0:T(8,128)(2,1)S(1)} %convert.16), channel_id=1, replica_groups=mesh['grp'=2,'tok'=4,'head'=4] {'tok'}, dimensions={2}, use_global_device_ids=true | all-gather | bytes 655360 | tf_op jit(solution)/shard_map/all_gather | solution.py:52
  42.6 7.0 %conditional.2 = (f32[256,1024]{1,0:T(8,128)S(1)}, f32[512,256]{1,0:T(8,128)}) conditional(s32[]{:T(128)} %convert_element_type.75, () %tuple.21, (bf16[192,1024]{1,0:T(8,128)(2,1)S(1)}, bf16[1024,256]{1,0:T(8,128)(2,1)S(1)}, bf16[1024,1]{0,1:T(2,128)(2,1)S(1)}, bf16[1024,256]{1,0:T(8,128)(2,1)S(1)}, bf16[1,512,256]{1,0,2:T(2,128)(2,1)}, ...), branch_computations={%region_1.0_spmd, %region_2.4_spmd} | conditional | flops 506758848 | bytes 14132096 | solution.py:99
  43.0 1.2 fusion.1
  46.0 1.4 multiply_convert_fusion.2
  48.6 1.1 fusion.12
  49.7 2.4 copy.18
  53.2 21.1 %reduce-scatter.13.cloned.1.call-done = f32[64,512]{1,0:T(8,128)} async-done(((f32[256,512]{1,0:T(8,128)}), f32[64,512]{1,0:T(8,128)}) %reduce-scatter.13.cloned.1.call-update) | async-done | bytes 131088
  75.6 15.5 %all_gather.21 = bf16[512,256]{0,1:T(8,128)(2,1)S(1)} all-gather(bf16[512,64]{0,1:T(8,128)(2,1)S(1)} %copy.14), channel_id=1, replica_groups=mesh['grp'=2,'tok'=4,'head'=4] {'tok'}, dimensions={1}, use_global_device_ids=true | all-gather | bytes 327680 | tf_op jit(solution)/shard_map/all_gather | solution.py:113
  91.9 11.3 %reduce-scatter.9.cloned.1.call-done = f32[256,256]{1,0:T(8,128)} async-done(((f32[256,1024]{1,0:T(8,128)}), f32[256,256]{1,0:T(8,128)}) %reduce-scatter.9.cloned.1.call-update) | async-done | bytes 262160 | tf_op jit(solution)/shard_map/reduce_scatter | solution.py:100
  104.3 15.4 %all_gather.20 = bf16[256,1024]{1,0:T(8,128)(2,1)S(1)} all-gather(bf16[256,256]{1,0:T(8,128)(2,1)S(1)} %fusion.35), channel_id=1, replica_groups=mesh['grp'=2,'tok'=4,'head'=4] {'tok'}, dimensions={1}, use_global_device_ids=true | all-gather | bytes 655360 | tf_op jit(solution)/shard_map/all_gather | solution.py:112
  120.7 34.5 %all-reduce.8.cloned.1.call-done = (bf16[512,256]{0,1:T(8,128)(2,1)}, bf16[256,1024]{1,0:T(8,128)(2,1)}) async-done(((bf16[512,256]{0,1:T(8,128)(2,1)}, bf16[256,1024]{1,0:T(8,128)(2,1)}), (bf16[512,256]{0,1:T(8,128)(2,1)}, bf16[256,1024]{1,0:T(8,128)(2,1)})) %all-reduce.8.cloned.1.call-update) | async-done | bytes 786448 | tf_op jit(solution)/shard_map/psum | solution.py:15
  155.2 4.4 %conditional.3 = (f32[256,1024]{1,0:T(8,128)S(1)}, f32[512,256]{1,0:T(8,128)}) conditional(s32[]{:T(128)} %convert_element_type.75, () %tuple.23, (bf16[192,1024]{1,0:T(8,128)(2,1)S(1)}, bf16[1024,256]{1,0:T(8,128)(2,1)S(1)}, bf16[1024,1]{0,1:T(2,128)(2,1)S(1)}, bf16[1024,256]{1,0:T(8,128)(2,1)S(1)}, bf16[512,256]{0,1:T(8,128)(2,1)}, ...), branch_computations={%region_15.16_spmd, %region_16.18_spmd} | conditional | flops 506758848 | bytes 11772744 | solution.py:99
  158.4 1.1 fusion.24
  159.5 2.4 copy.20
  162.6 1.4 multiply_reduce_fusion.7
  164.4 19.5 %reduce-scatter.15.cloned.1.call-done = f32[64,512]{1,0:T(8,128)} async-done(((f32[256,512]{1,0:T(8,128)}), f32[64,512]{1,0:T(8,128)}) %reduce-scatter.15.cloned.1.call-update) | async-done | bytes 131088
  185.2 15.6 %all_gather.23 = bf16[512,256]{0,1:T(8,128)(2,1)S(1)} all-gather(bf16[512,64]{0,1:T(8,128)(2,1)S(1)} %copy.16), channel_id=1, replica_groups=mesh['grp'=2,'tok'=4,'head'=4] {'tok'}, dimensions={1}, use_global_device_ids=true | all-gather | bytes 327680 | tf_op jit(solution)/shard_map/all_gather | solution.py:113
  201.6 11.1 %reduce-scatter.11.cloned.1.call-done = f32[256,256]{1,0:T(8,128)} async-done(((f32[256,1024]{1,0:T(8,128)}), f32[256,256]{1,0:T(8,128)}) %reduce-scatter.11.cloned.1.call-update) | async-done | bytes 262160 | tf_op jit(solution)/shard_map/reduce_scatter | solution.py:100
  213.8 15.8 %all_gather.22 = bf16[256,1024]{1,0:T(8,128)(2,1)S(1)} all-gather(bf16[256,256]{1,0:T(8,128)(2,1)S(1)} %multiply_convert_fusion.15), channel_id=1, replica_groups=mesh['grp'=2,'tok'=4,'head'=4] {'tok'}, dimensions={1}, use_global_device_ids=true | all-gather | bytes 655360 | tf_op jit(solution)/shard_map/all_gather | solution.py:112
  232.7 32.0 %all-reduce.6.cloned.1.call-done = (bf16[512,256]{0,1:T(8,128)(2,1)}, bf16[256,1024]{1,0:T(8,128)(2,1)}) async-done(((bf16[512,256]{0,1:T(8,128)(2,1)}, bf16[256,1024]{1,0:T(8,128)(2,1)}), (bf16[512,256]{0,1:T(8,128)(2,1)}, bf16[256,1024]{1,0:T(8,128)(2,1)})) %all-reduce.6.cloned.1.call-update) | async-done | bytes 786448 | tf_op jit(solution)/shard_map/psum | solution.py:15
  264.7 1.4 fusion.43
  266.5 6.4 %all-reduce = (f32[192]{0:T(256)S(1)}, f32[192]{0:T(256)S(1)}) all-reduce(f32[192]{0:T(256)S(1)} %get-tuple-element.95, f32[192]{0:T(256)S(1)} %get-tuple-element.97), channel_id=1, replica_groups=mesh['grp'=2,'tok'=4,'head'=4] {'head'}, use_global_device_ids=true, to_apply=%region_25.26 | all-reduce | flops 384 | bytes 3072 | tf_op jit(solution)/shard_map/psum | solution.py:117
  (102 shorter events, 20.7 us)
Async XLA Ops:
  6.5 156.1 %copy-start = (bf16[1024,256]{1,0:T(8,128)(2,1)S(1)}, bf16[1024,256]{1,0:T(8,128)(2,1)}, u32[]{:S(2)}) copy-start(bf16[1024,256]{1,0:T(8,128)(2,1)} %param.13) | copy-start | bytes 1572868
  6.5 67.8 %reduce-scatter.13.cloned.1.call-start = ((), (), s32[]{:S(2)}) async-start(), calls=%async_computation.6 | async-start | bytes 655360
  6.5 1.2 copy-start.12
  7.9 18.2 %copy-start.1 = (f32[1,256,256]{2,1,0:T(8,128)S(1)}, f32[1,256,256]{2,1,0:T(8,128)}, u32[]{:S(2)}) copy-start(f32[1,256,256]{2,1,0:T(8,128)} %param.17) | copy-start | bytes 786436
  7.9 34.7 %copy-start.16 = (bf16[1024,1]{0,1:T(2,128)(2,1)S(1)}, bf16[1024,1]{0,1:T(2,128)(2,1)}, u32[]{:S(2)}) copy-start(bf16[1024,1]{0,1:T(2,128)(2,1)} %param.16) | copy-start | bytes 6148
  26.1 16.5 %copy-start.5 = (bf16[1024,256]{1,0:T(8,128)(2,1)S(1)}, bf16[1024,256]{1,0:T(8,128)(2,1)}, u32[]{:S(2)}) copy-start(bf16[1024,256]{1,0:T(8,128)(2,1)} %param.14) | copy-start | bytes 1572868
  26.1 16.5 %copy-start.6 = (bf16[1024,256]{1,0:T(8,128)(2,1)S(1)}, bf16[1024,256]{1,0:T(8,128)(2,1)}, u32[]{:S(2)}) copy-start(bf16[1024,256]{1,0:T(8,128)(2,1)} %param.15) | copy-start | bytes 1572868
  44.4 1.1 copy-start.7
  44.8 1.2 copy-start.14
  47.4 1.1 copy-start.11
  47.4 1.1 copy-start.15
  49.7 2.5 copy-start.2
  52.1 51.1 %reduce-scatter.9.cloned.1.call-start = ((), (), s32[]{:S(2)}) async-start(), calls=%async_computation.4 | async-start | bytes 1310720 | tf_op jit(solution)/shard_map/reduce_scatter | solution.py:100
  52.9 102.3 %all-reduce.8.cloned.1.call-start = ((), (), s32[]{:S(2)}) async-start(), calls=%async_computation.9 | async-start | bytes 1572864 | tf_op jit(solution)/shard_map/psum | solution.py:15
  103.2 1.1 copy-start.4
  120.6 63.3 %reduce-scatter.15.cloned.1.call-start = ((), (), s32[]{:S(2)}) async-start(), calls=%async_computation.7 | async-start | bytes 655360
  155.2 1.0 copy-start.9
  156.8 1.0 copy-start.19
  159.5 2.5 copy-start.3
  162.0 50.7 %reduce-scatter.11.cloned.1.call-start = ((), (), s32[]{:S(2)}) async-start(), calls=%async_computation.5 | async-start | bytes 1310720 | tf_op jit(solution)/shard_map/reduce_scatter | solution.py:100
  162.5 1.5 copy-start.10
  162.6 102.2 %all-reduce.6.cloned.1.call-start = ((), (), s32[]{:S(2)}) async-start(), calls=%async_computation.8 | async-start | bytes 1572864 | tf_op jit(solution)/shard_map/psum | solution.py:15
  230.4 1.0 copy-start.8
  264.7 1.4 copy-start.20
  (3 other events, 2.5 us)
Sparse Core Ops, SparseCore 0:
  52.2 22.0 reduce-scatter.12
  76.6 26.4 reduce-scatter.8
  120.7 34.3 all-reduce.7
  162.1 21.8 reduce-scatter.14
  186.1 26.5 reduce-scatter.10
  230.5 34.1 all-reduce.5
where the time goes:
time: 282 us; the launch traced here: 281 us
  waiting for transfers between devices  131 us (46%)
  blocking collectives  103 us (37%)
  local copies, waits for them, and re-layouts  14.3 us (5%)
  between operations  13.7 us (5%)
  matrix products  12.1 us (4%)
  other arithmetic  6.49 us (2%)
    psum x2, waiting for transfers between devices, spread(): return lax.psum(kept, axis)  66.5 us
    unnamed x8, waiting for transfers between devices  42 us
    all_gather x2, blocking collectives, local(): lax.all_gather(part_in, 'tok', axis=1, tiled=True)  31.2 us
    all_gather x2, blocking collectives, local(): lax.all_gather(part_out, 'tok', axis=1, tiled=True)  31.2 us
    reduce_scatter x2, waiting for transfers between devices, local(): lax.psum_scatter(grads, 'tok', scatter_dimension=1, tiled=True)  22.4 us
    all_gather x1, blocking collectives, local(): lax.all_gather(fast_out, 'tok', axis=2, tiled=True)  18.1 us
    all_gather x1, blocking collectives, local(): lax.all_gather(fast_in, 'tok', axis=2, tiled=True)  16.5 us
    unnamed x36, local copies, waits for them, and re-layouts  9.64 us
  transfers between devices with their start and end apart: 6, of which 6 were waited for; matrix products, arithmetic and copies ran while one was open for 2% of the time, Pallas kernels for 0%

commit v1 on v0

--- a/solution.py
+++ b/solution.py
@@ -12,7 +12,11 @@
 
 def spread(value, axis, source):
     kept = jnp.where(lax.axis_index(axis) == source, value, 0).astype(value.dtype)
-    return lax.psum(kept, axis)
+
+    def number_the_joints(mat, axis_id):
+        return lax.all_gather(mat, axis_name=axis_id).sum(axis=0)
+
+    return number_the_joints(kept, axis)
 
 
 def rms_scale(values):

time: 282 us -> 267 us (0.947)
  waiting for transfers between devices: 131 us -> 93.6 us
  blocking collectives: 103 us -> 121 us
  other arithmetic: 6.49 us -> 11.6 us
    psum x2 -> x0, waiting for transfers between devices: 66.5 us -> none  [spread(): return lax.psum(kept, axis)]
    reduce_scatter x2, waiting for transfers between devices: 22.4 us -> 53.5 us  [local(): lax.psum_scatter(grads, 'tok', scatter_dimension=1, tiled=True)]
    all_gather x0 -> x2, blocking collectives: none -> 19.8 us  [number_the_joints(): return lax.all_gather(mat, axis_name=axis_id).sum(axis=0)]
    reduce_sum x0 -> x4, other arithmetic: none -> 6.48 us  [number_the_joints(): return lax.all_gather(mat, axis_name=axis_id).sum(axis=0)]
  transfers between devices with their start and end apart: 6 -> 6, of which waited for: 6 -> 4; matrix products, arithmetic and copies ran while one was open for 2% -> 4% of each run, Pallas kernels for 0% -> 0%
where the time goes in v1:
time: 267 us
  blocking collectives  121 us (45%)
  waiting for transfers between devices  93.6 us (35%)
  local copies, waits for them, and re-layouts  14.9 us (6%)
  between operations  13.7 us (5%)
  matrix products  11.7 us (4%)
  other arithmetic  11.6 us (4%)
    reduce_scatter x2, waiting for transfers between devices, local(): lax.psum_scatter(grads, 'tok', scatter_dimension=1, tiled=True)  53.5 us
    unnamed x8, waiting for transfers between devices  40.1 us
    all_gather x2, blocking collectives, local(): lax.all_gather(part_in, 'tok', axis=1, tiled=True)  31.9 us
    all_gather x2, blocking collectives, local(): lax.all_gather(part_out, 'tok', axis=1, tiled=True)  28.8 us
    all_gather x2, blocking collectives, number_the_joints(): return lax.all_gather(mat, axis_name=axis_id).sum(axis=0)  19.8 us
    all_gather x1, blocking collectives, local(): lax.all_gather(fast_out, 'tok', axis=2, tiled=True)  18.1 us
    all_gather x1, blocking collectives, local(): lax.all_gather(fast_in, 'tok', axis=2, tiled=True)  16.5 us
    unnamed x36, local copies, waits for them, and re-layouts  9.59 us
  transfers between devices with their start and end apart: 6, of which 4 were waited for; matrix products, arithmetic and copies ran while one was open for 4% of the time, Pallas kernels for 0%

profile of v1, /device:TPU:0, one launch (start us, length us, event | category | flops | bytes accessed | tf_op | source)
XLA Modules:
  0.0 266.7 jit_solution(4510759147636833709)
XLA Ops:
  6.5 1.2 slice_bitcast_fusion.1
  8.0 18.1 %all_gather.42 = bf16[1,512,256]{1,0,2:T(2,128)(2,1)} all-gather(bf16[1,512,64]{1,0,2:T(2,128)(2,1)S(1)} %copy.16), channel_id=1, replica_groups=mesh['grp'=2,'tok'=4,'head'=4] {'tok'}, dimensions={2}, use_global_device_ids=true | all-gather | bytes 327680 | tf_op jit(solution)/shard_map/all_gather | solution.py:57
  26.1 16.5 %all_gather.43 = bf16[1,256,1024]{2,1,0:T(8,128)(2,1)S(1)} all-gather(bf16[1,256,256]{2,1,0:T(8,128)(2,1)S(1)} %convert.20), channel_id=1, replica_groups=mesh['grp'=2,'tok'=4,'head'=4] {'tok'}, dimensions={2}, use_global_device_ids=true | all-gather | bytes 655360 | tf_op jit(solution)/shard_map/all_gather | solution.py:56
  42.6 7.0 %conditional.2 = (f32[256,1024]{1,0:T(8,128)S(1)}, f32[512,256]{1,0:T(8,128)}) conditional(s32[]{:T(128)} %convert_element_type.83, () %tuple.21, (bf16[192,1024]{1,0:T(8,128)(2,1)S(1)}, bf16[1024,256]{1,0:T(8,128)(2,1)S(1)}, bf16[1024,1]{0,1:T(2,128)(2,1)S(1)}, bf16[1024,256]{1,0:T(8,128)(2,1)S(1)}, bf16[1,512,256]{1,0,2:T(2,128)(2,1)}, ...), branch_computations={%region_1.0_spmd, %region_2.4_spmd} | conditional | flops 506758848 | bytes 13345608 | solution.py:103
  46.0 1.4 multiply_convert_fusion.2
  49.7 2.4 copy.23
  53.0 21.3 %reduce-scatter.13.cloned.1.call-done = f32[64,512]{1,0:T(8,128)} async-done(((f32[256,512]{1,0:T(8,128)}), f32[64,512]{1,0:T(8,128)}) %reduce-scatter.13.cloned.1.call-update) | async-done | bytes 131088
  75.4 26.8 %reduce-scatter.9.cloned.1.call-done = f32[256,256]{1,0:T(8,128)} async-done(((f32[256,1024]{1,0:T(8,128)}), f32[256,256]{1,0:T(8,128)}) %reduce-scatter.9.cloned.1.call-update) | async-done | bytes 262160 | tf_op jit(solution)/shard_map/reduce_scatter | solution.py:104
  103.4 16.0 %all_gather.44 = bf16[256,1024]{1,0:T(8,128)(2,1)S(1)} all-gather(bf16[256,256]{1,0:T(8,128)(2,1)S(1)} %fusion.35), channel_id=1, replica_groups=mesh['grp'=2,'tok'=4,'head'=4] {'tok'}, dimensions={1}, use_global_device_ids=true | all-gather | bytes 655360 | tf_op jit(solution)/shard_map/all_gather | solution.py:116
  121.0 14.4 %all_gather.47 = bf16[512,256]{0,1:T(8,128)(2,1)S(1)} all-gather(bf16[512,64]{0,1:T(8,128)(2,1)S(1)} %copy.19), channel_id=1, replica_groups=mesh['grp'=2,'tok'=4,'head'=4] {'tok'}, dimensions={1}, use_global_device_ids=true | all-gather | bytes 327680 | tf_op jit(solution)/shard_map/all_gather | solution.py:117
  135.4 10.0 %all-gather.1 = bf16[1024,256]{0,1:T(8,128)(2,1)S(1)} all-gather(bf16[512,256]{0,1:T(8,128)(2,1)S(1)} %broadcast_select_fusion.3), channel_id=3, replica_groups=mesh['grp'=2,'tok'=4,'head'=4] {'grp'}, dimensions={0}, use_global_device_ids=true | all-gather | bytes 786432 | tf_op jit(solution)/shard_map/all_gather | solution.py:17
  145.8 2.1 reduce_sum.162
  147.9 1.5 reduce_sum.159
  149.4 4.2 %conditional.3 = (f32[256,1024]{1,0:T(8,128)S(1)}, f32[512,256]{1,0:T(8,128)}) conditional(s32[]{:T(128)} %convert_element_type.83, () %tuple.23, (bf16[192,1024]{1,0:T(8,128)(2,1)S(1)}, bf16[1024,256]{1,0:T(8,128)(2,1)S(1)}, bf16[1024,1]{0,1:T(2,128)(2,1)S(1)}, bf16[1024,256]{1,0:T(8,128)(2,1)}, bf16[512,256]{0,1:T(8,128)(2,1)}, ...), branch_computations={%region_15.16_spmd, %region_16.18_spmd} | conditional | flops 506758848 | bytes 11772744 | solution.py:103
  153.6 2.4 copy.25
  156.7 2.0 multiply_reduce_fusion.7
  160.4 17.5 %reduce-scatter.15.cloned.1.call-done = f32[64,512]{1,0:T(8,128)} async-done(((f32[256,512]{1,0:T(8,128)}), f32[64,512]{1,0:T(8,128)}) %reduce-scatter.15.cloned.1.call-update) | async-done | bytes 131088
  179.0 26.6 %reduce-scatter.11.cloned.1.call-done = f32[256,256]{1,0:T(8,128)} async-done(((f32[256,1024]{1,0:T(8,128)}), f32[256,256]{1,0:T(8,128)}) %reduce-scatter.11.cloned.1.call-update) | async-done | bytes 262160 | tf_op jit(solution)/shard_map/reduce_scatter | solution.py:104
  206.7 16.0 %all_gather.50 = bf16[256,1024]{1,0:T(8,128)(2,1)S(1)} all-gather(bf16[256,256]{1,0:T(8,128)(2,1)S(1)} %multiply_convert_fusion.15), channel_id=1, replica_groups=mesh['grp'=2,'tok'=4,'head'=4] {'tok'}, dimensions={1}, use_global_device_ids=true | all-gather | bytes 655360 | tf_op jit(solution)/shard_map/all_gather | solution.py:116
  224.4 14.4 %all_gather.53 = bf16[512,256]{0,1:T(8,128)(2,1)S(1)} all-gather(bf16[512,64]{0,1:T(8,128)(2,1)S(1)} %copy.21), channel_id=1, replica_groups=mesh['grp'=2,'tok'=4,'head'=4] {'tok'}, dimensions={1}, use_global_device_ids=true | all-gather | bytes 327680 | tf_op jit(solution)/shard_map/all_gather | solution.py:117
  238.8 9.9 %all-gather.3 = bf16[1024,256]{0,1:T(8,128)(2,1)S(1)} all-gather(bf16[512,256]{0,1:T(8,128)(2,1)S(1)} %broadcast_select_fusion.2), channel_id=5, replica_groups=mesh['grp'=2,'tok'=4,'head'=4] {'grp'}, dimensions={0}, use_global_device_ids=true | all-gather | bytes 786432 | tf_op jit(solution)/shard_map/all_gather | solution.py:17
  249.0 1.4 reduce_sum.168
  250.5 1.5 reduce_sum.166
  252.7 5.7 %all-reduce = (f32[192]{0:T(256)S(1)}, f32[192]{0:T(256)S(1)}) all-reduce(f32[192]{0:T(256)S(1)} %get-tuple-element.97, f32[192]{0:T(256)S(1)} %get-tuple-element.99), channel_id=1, replica_groups=mesh['grp'=2,'tok'=4,'head'=4] {'head'}, use_global_device_ids=true, to_apply=%region_25.26 | all-reduce | flops 384 | bytes 3072 | tf_op jit(solution)/shard_map/psum | solution.py:121
  (106 shorter events, 23.7 us)
Async XLA Ops:
  6.5 150.2 %copy-start = (bf16[1024,256]{1,0:T(8,128)(2,1)S(1)}, bf16[1024,256]{1,0:T(8,128)(2,1)}, u32[]{:S(2)}) copy-start(bf16[1024,256]{1,0:T(8,128)(2,1)} %param.13) | copy-start | bytes 1572868
  6.5 67.8 %reduce-scatter.13.cloned.1.call-start = ((), (), s32[]{:S(2)}) async-start(), calls=%async_computation.8 | async-start | bytes 655360
  6.5 1.2 copy-start.11
  7.9 18.2 %copy-start.1 = (f32[1,256,256]{2,1,0:T(8,128)S(1)}, f32[1,256,256]{2,1,0:T(8,128)}, u32[]{:S(2)}) copy-start(f32[1,256,256]{2,1,0:T(8,128)} %param.17) | copy-start | bytes 786436
  7.9 34.7 %copy-start.15 = (bf16[1024,1]{0,1:T(2,128)(2,1)S(1)}, bf16[1024,1]{0,1:T(2,128)(2,1)}, u32[]{:S(2)}) copy-start(bf16[1024,1]{0,1:T(2,128)(2,1)} %param.16) | copy-start | bytes 6148
  26.1 16.5 %copy-start.5 = (bf16[1024,256]{1,0:T(8,128)(2,1)S(1)}, bf16[1024,256]{1,0:T(8,128)(2,1)}, u32[]{:S(2)}) copy-start(bf16[1024,256]{1,0:T(8,128)(2,1)} %param.14) | copy-start | bytes 1572868
  26.1 16.5 %copy-start.6 = (bf16[1024,256]{1,0:T(8,128)(2,1)S(1)}, bf16[1024,256]{1,0:T(8,128)(2,1)}, u32[]{:S(2)}) copy-start(bf16[1024,256]{1,0:T(8,128)(2,1)} %param.15) | copy-start | bytes 1572868
  44.4 1.1 copy-start.8
  47.4 1.1 copy-start.10
  49.7 2.5 copy-start.2
  52.1 50.1 %reduce-scatter.9.cloned.1.call-start = ((), (), s32[]{:S(2)}) async-start(), calls=%async_computation.4 | async-start | bytes 1310720 | tf_op jit(solution)/shard_map/reduce_scatter | solution.py:104
  52.9 95.0 %all-gather.7.cloned.1.call-start = ((), (), s32[]{:S(2)}) async-start(), calls=%async_computation.6 | async-start | bytes 1572864 | tf_op jit(solution)/shard_map/all_gather | solution.py:17
  102.2 1.1 copy-start.4
  120.2 57.8 %reduce-scatter.15.cloned.1.call-start = ((), (), s32[]{:S(2)}) async-start(), calls=%async_computation.9 | async-start | bytes 655360
  149.8 1.1 copy-start.7
  150.8 0.9 copy-start.13
  153.6 2.5 copy-start.3
  156.0 49.6 %reduce-scatter.11.cloned.1.call-start = ((), (), s32[]{:S(2)}) async-start(), calls=%async_computation.5 | async-start | bytes 1310720 | tf_op jit(solution)/shard_map/reduce_scatter | solution.py:104
  156.6 2.1 copy-start.9
  156.6 93.8 %all-gather.9.cloned.1.call-start = ((), (), s32[]{:S(2)}) async-start(), calls=%async_computation.7 | async-start | bytes 1572864 | tf_op jit(solution)/shard_map/all_gather | solution.py:17
  159.1 1.0 copy-start.12
  223.5 0.6 copy-start.17
  250.5 1.5 copy-start.14
  258.4 0.7 copy-start.18
  (1 other events, 0.5 us)
Sparse Core Ops, SparseCore 0:
  52.2 22.0 reduce-scatter.12
  76.6 25.5 reduce-scatter.8
  120.3 24.0 all-gather.6
  156.2 21.7 reduce-scatter.14
  180.1 25.4 reduce-scatter.10
  223.7 23.9 all-gather.8
